TPU v7x, 32 devices: a whole 2x2x4 slice. The times are simulated.
32 devices in a mesh: groups: 2 (over y), shots: 4 (over z), dom: 2 (over x), sub: 2 (over core).
Axes of the slice: x: 2, y: 2, z: 4, core: 2. Of those that a mesh axis runs over, the one named last changes fastest.
Arguments:
- velocity: float32 [64, 16, 256], P(('groups', 'shots'), 'dom', 'sub'), parts along dimension 0, may hold values from 0.15 to 0.4
- wave_prev: bfloat16 [8, 32, 16, 256], P(('groups', 'shots'), None, 'dom', 'sub'), parts along dimension 0, may hold values from -6 to 6
- wave_now: bfloat16 [8, 32, 16, 256], P(('groups', 'shots'), None, 'dom', 'sub'), parts along dimension 0, may hold values from -6 to 6
- adj_next: bfloat16 [8, 32, 16, 256], P(('groups', 'shots'), None, 'dom', 'sub'), parts along dimension 0, may hold values from -6 to 6
- adj_now: bfloat16 [8, 32, 16, 256], P(('groups', 'shots'), None, 'dom', 'sub'), parts along dimension 0, may hold values from -6 to 6
- sponge: int32 [32, 16, 256], P(None, 'dom', 'sub'), may hold values 0 or 1
- wavelet: float32 [8, 6], P(('groups', 'shots')), parts along dimension 0, may hold values from -12 to 12
- src_pos: int32 [8], P(('groups', 'shots')), parts along dimension 0, may hold values from 0 to 4095
- rec_pos: int32 [8, 256], P(('groups', 'shots')), parts along dimension 0, may hold values from 0 to 4095
- observed: float32 [8, 4, 256], P(('groups', 'shots')), parts along dimension 0, may hold values from -6 to 6
Outputs:
- direction: float32 [64, 16, 256], P(('groups', 'shots'), 'dom', 'sub'), parts along dimension 0
- wave_out: float32 [8, 32, 16, 256], P(('groups', 'shots'), None, 'dom', 'sub'), parts along dimension 0
There are 2 independent parts, one for each index of `groups`. A program takes and returns all parts, laid end to end along the dimension named above; an argument that names none is the same for every part. Nothing has to cross between parts.
Inputs may be any that keep to these rules, and one draw needn't show every extreme that they name: `src_pos`: a horizontal position x * 256 + y on the grid. `rec_pos`: horizontal positions x * 256 + y on the grid, possibly repeated.
All inputs are finite; a program needn't handle non-finite values. Where the computation divides by a largest or mean magnitude, that divisor is 1e-20 or more. No bound on the sum of `sponge` on one device may be relied on, other than what follows from the above.
Results may differ from a plain program's by a relative error of at most 0.0003.
Values sent between devices are 32-bit elements; how exact they have to be, the bound alone decides.
A program may use at most 64 MiB of HBM per device.

v0:
```python
import jax
import jax.numpy as jnp
from jax import lax
from jax.sharding import PartitionSpec as P

NF = 4
NFIN = 2
coeffs = (-205.0 / 72.0, 8.0 / 5.0, -1.0 / 5.0, 8.0 / 315.0, -1.0 / 560.0)
damp_rate = 0.2
step_rate = 0.1
floor_share = 0.5
src_depth = 2
rec_depth = 1
reach = 4


def padded_2(cells, sides, width):
    for axis, dim in sides:
        count = lax.axis_size(axis)
        ends = count - 1
        head = lax.slice_in_dim(cells, 0, width, axis=dim)
        tail = lax.slice_in_dim(cells, cells.shape[dim] - width, cells.shape[dim], axis=dim)
        cells = jnp.concatenate(
            [
                lax.ppermute(tail, axis, [(i, (i + 1) % count) for i in range(ends)]),
                cells,
                lax.ppermute(head, axis, [((i + 1) % count, i) for i in range(ends)]),
            ],
            axis=dim,
        )
    return cells


def laplace(padded, depth, rows, cols):
    z0, x0, y0 = (reach, reach, reach)
    total = 3.0 * coeffs[0] * padded[z0 : z0 + depth, x0 : x0 + rows, y0 : y0 + cols]
    for offset in range(1, 5):
        pair = padded[z0 + offset : z0 + offset + depth, x0 : x0 + rows, y0 : y0 + cols]
        pair = pair + padded[z0 - offset : z0 - offset + depth, x0 : x0 + rows, y0 : y0 + cols]
        pair = pair + padded[z0 : z0 + depth, x0 + offset : x0 + offset + rows, y0 : y0 + cols]
        pair = pair + padded[z0 : z0 + depth, x0 - offset : x0 - offset + rows, y0 : y0 + cols]
        pair = pair + padded[z0 : z0 + depth, x0 : x0 + rows, y0 + offset : y0 + offset + cols]
        pair = pair + padded[z0 : z0 + depth, x0 : x0 + rows, y0 - offset : y0 - offset + cols]
        total = total + coeffs[offset] * pair
    return total


def advance(now, before, kappa, damp, plane, level):
    widened = padded_2(now, (("dom", 1), ("sub", 2)), 4)
    padded = jnp.pad(widened, ((reach, reach), (0, 0), (0, 0)))
    lap = laplace(padded, now.shape[0], now.shape[1], now.shape[2])
    numer = 2.0 * now - (1.0 - damp) * before + kappa * lap
    numer = numer.at[level].add(plane)
    return numer / (1.0 + damp)


def local_spots(positions, rows, cols):
    cols_all = cols * lax.axis_size("sub")
    gx = positions // cols_all
    gy = positions % cols_all
    local_x = gx - lax.axis_index("dom") * rows
    local_y = gy - lax.axis_index("sub") * cols
    inside = (local_x >= 0) & (local_x < rows) & (local_y >= 0) & (local_y < cols)
    spots = jnp.where(inside, local_x * cols + local_y, 0)
    return (spots, inside)


def place_local(spots, inside, values, rows, cols):
    kept = jnp.where(inside, values, 0.0)
    flat = jnp.zeros((rows * cols,), jnp.float32).at[spots].add(kept)
    return flat.reshape(rows, cols)


def shards(
    velocity, wave_prev, wave_now, adj_next, adj_now, sponge, wavelet, src_pos, rec_pos, observed
):
    depth, rows, cols = sponge.shape
    full_vel = lax.all_gather(velocity, "shots", axis=0, tiled=True)
    kappa = full_vel * full_vel
    damp = damp_rate * sponge.astype(jnp.float32)
    amps = wavelet[0]
    src_spot, src_inside = local_spots(src_pos, rows, cols)
    rec_spot, rec_inside = local_spots(rec_pos[0], rows, cols)
    states = [wave_prev[0].astype(jnp.float32), wave_now[0].astype(jnp.float32)]
    for step in range(NF):
        plane = place_local(src_spot, src_inside, amps[step][None], rows, cols)
        states.append(advance(states[-1], states[-2], kappa, damp, plane, src_depth))
    lam_after = adj_next[0].astype(jnp.float32)
    lam_now = adj_now[0].astype(jnp.float32)
    grad = jnp.zeros_like(kappa)
    for level in range(NF, 0, -1):
        sampled = states[level + 1][rec_depth].reshape(-1)[rec_spot]
        resid = sampled - observed[0, level - 1]
        plane = place_local(rec_spot, rec_inside, resid, rows, cols)
        lam_before = advance(lam_now, lam_after, kappa, damp, plane, rec_depth)
        lower = level - 1
        accel = states[lower + 2] - 2.0 * states[lower + 1] + states[lower]
        grad = grad + lam_before * accel
        lam_after, lam_now = (lam_now, lam_before)
    illum = jnp.zeros_like(kappa)
    for level in range(1, NF + 1):
        illum = illum + states[level + 1] * states[level + 1]
    shot_count = lax.axis_size("shots")
    grad_all, illum_all = lax.psum((grad, illum), "shots")
    precond = grad_all / (illum_all + floor_share * shot_count)
    peak = lax.pmax(jnp.max(jnp.abs(precond)), ("dom", "sub"))
    full_dir = precond / (peak + 1e-06)
    updated = full_vel * (1.0 - step_rate * full_dir)
    owned = velocity.shape[0]
    direction = lax.dynamic_slice_in_dim(full_dir, lax.axis_index("shots") * owned, owned, 0)
    kappa_new = updated * updated
    before, current = (states[-2], states[-1])
    for step in range(NFIN):
        plane = place_local(src_spot, src_inside, amps[NF + step][None], rows, cols)
        following = advance(current, before, kappa_new, damp, plane, src_depth)
        before, current = (current, following)
    return (direction, current[None])


def solution(mesh):
    return jax.shard_map(
        shards,
        mesh=mesh,
        in_specs=(
            P(("groups", "shots"), "dom", "sub"),
            P(("groups", "shots"), None, "dom", "sub"),
            P(("groups", "shots"), None, "dom", "sub"),
            P(("groups", "shots"), None, "dom", "sub"),
            P(("groups", "shots"), None, "dom", "sub"),
            P(None, "dom", "sub"),
            P(("groups", "shots"), None),
            P(("groups", "shots")),
            P(("groups", "shots"), None),
            P(("groups", "shots"), None, None),
        ),
        out_specs=(
            P(("groups", "shots"), "dom", "sub"),
            P(("groups", "shots"), None, "dom", "sub"),
        ),
        check_vma=False,
    )
```

profile of v0, /device:TPU:0, one launch (start us, length us, event | category | flops | bytes accessed | tf_op | source)
XLA Modules:
  0.0 231.8 jit_solution(6835556315163786703)
XLA Ops:
  8.1 4.9 %collective-permute-start.4 = (f32[32,4,128]{2,1,0:T(4,128)S(1)}, f32[32,4,128]{2,1,0:T(4,128)S(1)}, u32[]{:S(2)}, u32[]{:S(2)}) collective-permute-start(f32[32,4,128]{2,1,0:T(4,128)S(1)} %get-tuple-element.261), channel_id=1, source_target_pairs={{0,2},{1,3},{4,6},{5,7},{8,10},{9,11},{12,14},{13,15},{16,18},{17,... | collective-permute-start | bytes 196616 | tf_op jit(solution)/shard_map/ppermute | solution.py:25
  14.3 4.5 %collective-permute-start = (f32[32,4,128]{2,1,0:T(4,128)S(1)}, f32[32,4,128]{2,1,0:T(4,128)S(1)}, u32[]{:S(2)}, u32[]{:S(2)}) collective-permute-start(f32[32,4,128]{2,1,0:T(4,128)S(1)} %get-tuple-element.251), channel_id=1, source_target_pairs={{0,2},{1,3},{4,6},{5,7},{8,10},{9,11},{12,14},{13,15},{16,18},{17,... | collective-permute-start | bytes 196616 | tf_op jit(solution)/shard_map/ppermute | solution.py:25
  27.0 2.6 %fusion.344 = f32[1024]{0:T(1024)S(1)} fusion(f32[1024]{0:T(1024)S(1)} %broadcast.395.clone, s32[]{:T(128)} %bitcast.12, pred[1]{0:T(512)(128)(4,1)} %get-tuple-element.275, f32[1,1]{1,0:T(1,128)} %get-tuple-element.270, s32[1]{0:T(128)} %compare_select_fusion.1), kind=kLoop, calls=%fused_computation.685 | loop fusion | flops 5 | bytes 525 | tf_op jit(solution)/shard_map/scatter-add | solution.py:70
  29.6 2.6 %fusion.342 = f32[1024]{0:T(1024)S(1)} fusion(f32[1024]{0:T(1024)S(1)} %broadcast.395.clone.1, s32[]{:T(128)} %bitcast.12, pred[1]{0:T(512)(128)(4,1)} %get-tuple-element.275, f32[1,1]{1,0:T(1,128)} %get-tuple-element.269, s32[1]{0:T(128)} %compare_select_fusion.1), kind=kLoop, calls=%fused_computation.682 | loop fusion | flops 5 | bytes 525 | tf_op jit(solution)/shard_map/scatter-add | solution.py:70
  32.3 2.6 %fusion.340 = f32[1024]{0:T(1024)S(1)} fusion(f32[1024]{0:T(1024)S(1)} %broadcast.395.clone.2, s32[]{:T(128)} %bitcast.12, pred[1]{0:T(512)(128)(4,1)} %get-tuple-element.275, f32[1,1]{1,0:T(1,128)} %get-tuple-element.268, s32[1]{0:T(128)} %compare_select_fusion.1), kind=kLoop, calls=%fused_computation.679 | loop fusion | flops 5 | bytes 525 | tf_op jit(solution)/shard_map/scatter-add | solution.py:70
  34.9 2.6 %fusion.338 = f32[1024]{0:T(1024)S(1)} fusion(f32[1024]{0:T(1024)S(1)} %broadcast.395.clone.3, s32[]{:T(128)} %bitcast.12, pred[1]{0:T(512)(128)(4,1)} %get-tuple-element.275, f32[1,1]{1,0:T(1,128)} %get-tuple-element.267, s32[1]{0:T(128)} %compare_select_fusion.1), kind=kLoop, calls=%fused_computation.676 | loop fusion | flops 5 | bytes 525 | tf_op jit(solution)/shard_map/scatter-add | solution.py:70
  37.5 13.6 %all_gather.3 = f32[32,8,128]{2,1,0:T(8,128)S(1)} all-gather(f32[8,8,128]{2,1,0:T(8,128)S(1)} %copy-done.7), channel_id=1, replica_groups=mesh['groups'=2,'shots'=4,'dom'=2,'sub'=2] {'shots'}, dimensions={0}, use_global_device_ids=true | all-gather | bytes 163840 | tf_op jit(solution)/shard_map/all_gather | solution.py:78
  54.1 3.1 %collective-permute-start.2 = (f32[32,16,4]{2,1,0:T(8,128)S(1)}, f32[32,16,4]{2,1,0:T(8,128)S(1)}, u32[]{:S(2)}, u32[]{:S(2)}) collective-permute-start(f32[32,16,4]{2,1,0:T(8,128)S(1)} %get-tuple-element.221), channel_id=1, source_target_pairs={{0,1},{2,3},{4,5},{6,7},{8,9},{10,11},{12,13},{14,15},{16,17},{18,... | collective-permute-start | bytes 24584 | tf_op jit(solution)/shard_map/ppermute | solution.py:25
  60.5 4.5 %collective-permute-start.8 = (f32[32,4,128]{2,1,0:T(4,128)S(1)}, f32[32,4,128]{2,1,0:T(4,128)S(1)}, u32[]{:S(2)}, u32[]{:S(2)}) collective-permute-start(f32[32,4,128]{2,1,0:T(4,128)S(1)} %get-tuple-element.259), channel_id=1, source_target_pairs={{0,2},{1,3},{4,6},{5,7},{8,10},{9,11},{12,14},{13,15},{16,18},{17,... | collective-permute-start | bytes 196616 | tf_op jit(solution)/shard_map/ppermute | solution.py:25
  67.3 4.5 %collective-permute-done.9 = f32[32,4,128]{2,1,0:T(4,128)S(1)} collective-permute-done((f32[32,4,128]{2,1,0:T(4,128)S(1)}, f32[32,4,128]{2,1,0:T(4,128)S(1)}, u32[]{:S(2)}, u32[]{:S(2)}) %collective-permute-start.9) | collective-permute-done | bytes 65568 | tf_op jit(solution)/shard_map/ppermute | solution.py:27
  83.0 3.5 %collective-permute-done.13 = f32[32,4,128]{2,1,0:T(4,128)S(1)} collective-permute-done((f32[32,4,128]{2,1,0:T(4,128)S(1)}, f32[32,4,128]{2,1,0:T(4,128)S(1)}, u32[]{:S(2)}, u32[]{:S(2)}) %collective-permute-start.13) | collective-permute-done | bytes 65568 | tf_op jit(solution)/shard_map/ppermute | solution.py:27
  97.1 3.5 %collective-permute-done.17 = f32[32,4,128]{2,1,0:T(4,128)S(1)} collective-permute-done((f32[32,4,128]{2,1,0:T(4,128)S(1)}, f32[32,4,128]{2,1,0:T(4,128)S(1)}, u32[]{:S(2)}, u32[]{:S(2)}) %collective-permute-start.17) | collective-permute-done | bytes 65568 | tf_op jit(solution)/shard_map/ppermute | solution.py:27
  109.0 2.3 %scatter_custom_fusion = f32[1024]{0:T(1024)S(1)} fusion(s32[256]{0:T(256)S(1)} %bitcast.109, f32[256]{0:T(256)S(1)} %get-tuple-element.274, f32[]{:T(128)} %constant.405.clone.1), kind=kCustom, calls=%fused_computation.646 | custom fusion | flops 256 | bytes 4100 | tf_op jit(solution)/shard_map/scatter-add | solution.py:70
  115.1 4.1 %collective-permute-done.21 = f32[32,4,128]{2,1,0:T(4,128)S(1)} collective-permute-done((f32[32,4,128]{2,1,0:T(4,128)S(1)}, f32[32,4,128]{2,1,0:T(4,128)S(1)}, u32[]{:S(2)}, u32[]{:S(2)}) %collective-permute-start.21) | collective-permute-done | bytes 65568 | tf_op jit(solution)/shard_map/ppermute | solution.py:27
  122.1 2.3 %scatter_custom_fusion.1 = f32[1024]{0:T(1024)S(1)} fusion(s32[256]{0:T(256)S(1)} %bitcast.110, f32[256]{0:T(256)S(1)} %get-tuple-element.273, f32[]{:T(128)} %constant.405.clone.1), kind=kCustom, calls=%fused_computation.644 | custom fusion | flops 256 | bytes 4100 | tf_op jit(solution)/shard_map/scatter-add | solution.py:70
  129.7 4.5 %collective-permute-done.25 = f32[32,4,128]{2,1,0:T(4,128)S(1)} collective-permute-done((f32[32,4,128]{2,1,0:T(4,128)S(1)}, f32[32,4,128]{2,1,0:T(4,128)S(1)}, u32[]{:S(2)}, u32[]{:S(2)}) %collective-permute-start.25) | collective-permute-done | bytes 65568 | tf_op jit(solution)/shard_map/ppermute | solution.py:27
  140.0 2.3 %scatter_custom_fusion.2 = f32[1024]{0:T(1024)S(1)} fusion(s32[256]{0:T(256)S(1)} %bitcast.112, f32[256]{0:T(256)S(1)} %get-tuple-element.272, f32[]{:T(128)} %constant.405.clone.1), kind=kCustom, calls=%fused_computation.642 | custom fusion | flops 256 | bytes 4100 | tf_op jit(solution)/shard_map/scatter-add | solution.py:70
  146.6 4.5 %collective-permute-start.32 = (f32[32,4,128]{2,1,0:T(4,128)S(1)}, f32[32,4,128]{2,1,0:T(4,128)S(1)}, u32[]{:S(2)}, u32[]{:S(2)}) collective-permute-start(f32[32,4,128]{2,1,0:T(4,128)S(1)} %get-tuple-element.253), channel_id=1, source_target_pairs={{0,2},{1,3},{4,6},{5,7},{8,10},{9,11},{12,14},{13,15},{16,18},{17,... | collective-permute-start | bytes 196616 | tf_op jit(solution)/shard_map/ppermute | solution.py:25
  152.7 2.3 %collective-permute-start.30 = (f32[32,16,4]{2,1,0:T(8,128)S(1)}, f32[32,16,4]{2,1,0:T(8,128)S(1)}, u32[]{:S(2)}, u32[]{:S(2)}) collective-permute-start(f32[32,16,4]{2,1,0:T(8,128)S(1)} %get-tuple-element.209), channel_id=1, source_target_pairs={{0,1},{2,3},{4,5},{6,7},{8,9},{10,11},{12,13},{14,15},{16,17},{18,... | collective-permute-start | bytes 24584 | tf_op jit(solution)/shard_map/ppermute | solution.py:25
  164.2 2.6 %fusion.336 = f32[1024]{0:T(1024)S(1)} fusion(f32[1024]{0:T(1024)S(1)} %broadcast.395.clone.4, s32[]{:T(128)} %bitcast.12, pred[1]{0:T(512)(128)(4,1)} %get-tuple-element.275, f32[1,1]{1,0:T(1,128)} %get-tuple-element.271, s32[1]{0:T(128)} %compare_select_fusion.1), kind=kLoop, calls=%fused_computation.673 | loop fusion | flops 5 | bytes 525 | tf_op jit(solution)/shard_map/scatter-add | solution.py:70
  167.1 31.3 %all-reduce.13.cloned.1.call-done = (f32[32,8,128]{2,1,0:T(8,128)}, f32[32,8,128]{2,1,0:T(8,128)}) async-done(((f32[32,8,128]{2,1,0:T(8,128)}, f32[32,8,128]{2,1,0:T(8,128)}), (f32[32,8,128]{2,1,0:T(8,128)}, f32[32,8,128]{2,1,0:T(8,128)})) %all-reduce.13.cloned.1.call-update) | async-done | bytes 262160 | tf_op jit(solution)/shard_map/psum | solution.py:104
  200.4 6.3 %pmax.7 = f32[]{:T(128)} all-reduce(f32[]{:T(128)} %abs_reduce_fusion), channel_id=1, replica_groups=mesh['groups'=2,'shots'=4,'dom'=2,'sub'=2] {'dom','sub'}, use_global_device_ids=true, to_apply=%region_7.8 | all-reduce | flops 1 | bytes 8 | tf_op jit(solution)/shard_map/pmax | solution.py:106
  208.1 3.6 %collective-permute-start.36 = (f32[32,4,128]{2,1,0:T(4,128)S(1)}, f32[32,4,128]{2,1,0:T(4,128)S(1)}, u32[]{:S(2)}, u32[]{:S(2)}) collective-permute-start(f32[32,4,128]{2,1,0:T(4,128)S(1)} %get-tuple-element.243), channel_id=1, source_target_pairs={{0,2},{1,3},{4,6},{5,7},{8,10},{9,11},{12,14},{13,15},{16,18},{17,... | collective-permute-start | bytes 196616 | tf_op jit(solution)/shard_map/ppermute | solution.py:25
  213.1 2.6 %fusion.334 = f32[1024]{0:T(1024)S(1)} fusion(f32[1024]{0:T(1024)S(1)} %broadcast.395.clone.5, s32[]{:T(128)} %bitcast.12, pred[1]{0:T(512)(128)(4,1)} %get-tuple-element.275, f32[1,1]{1,0:T(1,128)} %get-tuple-element.266, s32[1]{0:T(128)} %compare_select_fusion.1), kind=kLoop, calls=%fused_computation.670 | loop fusion | flops 5 | bytes 525 | tf_op jit(solution)/shard_map/scatter-add | solution.py:70
  (198 shorter events, 90.9 us)
Async XLA Ops:
  7.2 191.2 %all-reduce.13.cloned.1.call-start = ((), (), s32[]{:S(2)}) async-start(), calls=%async_computation | async-start | bytes 524288 | tf_op jit(solution)/shard_map/psum | solution.py:104
  8.1 43.0 %collective-permute-start.4 = (f32[32,4,128]{2,1,0:T(4,128)S(1)}, f32[32,4,128]{2,1,0:T(4,128)S(1)}, u32[]{:S(2)}, u32[]{:S(2)}) collective-permute-start(f32[32,4,128]{2,1,0:T(4,128)S(1)} %get-tuple-element.261), channel_id=1, source_target_pairs={{0,2},{1,3},{4,6},{5,7},{8,10},{9,11},{12,14},{13,15},{16,18},{17,... | collective-permute-start | bytes 196616 | tf_op jit(solution)/shard_map/ppermute | solution.py:25
  13.0 38.1 %collective-permute-start.5 = (f32[32,4,128]{2,1,0:T(4,128)S(1)}, f32[32,4,128]{2,1,0:T(4,128)S(1)}, u32[]{:S(2)}, u32[]{:S(2)}) collective-permute-start(f32[32,4,128]{2,1,0:T(4,128)S(1)} %get-tuple-element.260), channel_id=1, source_target_pairs={{2,0},{3,1},{6,4},{7,5},{10,8},{11,9},{14,12},{15,13},{18,16},{19,... | collective-permute-start | bytes 196616 | tf_op jit(solution)/shard_map/ppermute | solution.py:27
  14.3 39.5 %collective-permute-start = (f32[32,4,128]{2,1,0:T(4,128)S(1)}, f32[32,4,128]{2,1,0:T(4,128)S(1)}, u32[]{:S(2)}, u32[]{:S(2)}) collective-permute-start(f32[32,4,128]{2,1,0:T(4,128)S(1)} %get-tuple-element.251), channel_id=1, source_target_pairs={{0,2},{1,3},{4,6},{5,7},{8,10},{9,11},{12,14},{13,15},{16,18},{17,... | collective-permute-start | bytes 196616 | tf_op jit(solution)/shard_map/ppermute | solution.py:25
  18.9 35.0 %collective-permute-start.1 = (f32[32,4,128]{2,1,0:T(4,128)S(1)}, f32[32,4,128]{2,1,0:T(4,128)S(1)}, u32[]{:S(2)}, u32[]{:S(2)}) collective-permute-start(f32[32,4,128]{2,1,0:T(4,128)S(1)} %get-tuple-element.250), channel_id=1, source_target_pairs={{2,0},{3,1},{6,4},{7,5},{10,8},{11,9},{14,12},{15,13},{18,16},{19,... | collective-permute-start | bytes 196616 | tf_op jit(solution)/shard_map/ppermute | solution.py:27
  51.3 7.2 %collective-permute-start.6 = (f32[32,16,4]{2,1,0:T(8,128)S(1)}, f32[32,16,4]{2,1,0:T(8,128)S(1)}, u32[]{:S(2)}, u32[]{:S(2)}) collective-permute-start(f32[32,16,4]{2,1,0:T(8,128)S(1)} %get-tuple-element.241), channel_id=1, source_target_pairs={{0,1},{2,3},{4,5},{6,7},{8,9},{10,11},{12,13},{14,15},{16,17},{18,... | collective-permute-start | bytes 24584 | tf_op jit(solution)/shard_map/ppermute | solution.py:25
  52.6 5.9 %collective-permute-start.7 = (f32[32,16,4]{2,1,0:T(8,128)S(1)}, f32[32,16,4]{2,1,0:T(8,128)S(1)}, u32[]{:S(2)}, u32[]{:S(2)}) collective-permute-start(f32[32,16,4]{2,1,0:T(8,128)S(1)} %get-tuple-element.240), channel_id=1, source_target_pairs={{1,0},{3,2},{5,4},{7,6},{9,8},{11,10},{13,12},{15,14},{17,16},{19,... | collective-permute-start | bytes 24584 | tf_op jit(solution)/shard_map/ppermute | solution.py:27
  54.1 12.2 %collective-permute-start.2 = (f32[32,16,4]{2,1,0:T(8,128)S(1)}, f32[32,16,4]{2,1,0:T(8,128)S(1)}, u32[]{:S(2)}, u32[]{:S(2)}) collective-permute-start(f32[32,16,4]{2,1,0:T(8,128)S(1)} %get-tuple-element.221), channel_id=1, source_target_pairs={{0,1},{2,3},{4,5},{6,7},{8,9},{10,11},{12,13},{14,15},{16,17},{18,... | collective-permute-start | bytes 24584 | tf_op jit(solution)/shard_map/ppermute | solution.py:25
  57.2 9.2 %collective-permute-start.3 = (f32[32,16,4]{2,1,0:T(8,128)S(1)}, f32[32,16,4]{2,1,0:T(8,128)S(1)}, u32[]{:S(2)}, u32[]{:S(2)}) collective-permute-start(f32[32,16,4]{2,1,0:T(8,128)S(1)} %get-tuple-element.220), channel_id=1, source_target_pairs={{1,0},{3,2},{5,4},{7,6},{9,8},{11,10},{13,12},{15,14},{17,16},{19,... | collective-permute-start | bytes 24584 | tf_op jit(solution)/shard_map/ppermute | solution.py:27
  60.5 6.9 %collective-permute-start.8 = (f32[32,4,128]{2,1,0:T(4,128)S(1)}, f32[32,4,128]{2,1,0:T(4,128)S(1)}, u32[]{:S(2)}, u32[]{:S(2)}) collective-permute-start(f32[32,4,128]{2,1,0:T(4,128)S(1)} %get-tuple-element.259), channel_id=1, source_target_pairs={{0,2},{1,3},{4,6},{5,7},{8,10},{9,11},{12,14},{13,15},{16,18},{17,... | collective-permute-start | bytes 196616 | tf_op jit(solution)/shard_map/ppermute | solution.py:25
  65.0 6.7 %collective-permute-start.9 = (f32[32,4,128]{2,1,0:T(4,128)S(1)}, f32[32,4,128]{2,1,0:T(4,128)S(1)}, u32[]{:S(2)}, u32[]{:S(2)}) collective-permute-start(f32[32,4,128]{2,1,0:T(4,128)S(1)} %get-tuple-element.258), channel_id=1, source_target_pairs={{2,0},{3,1},{6,4},{7,5},{10,8},{11,9},{14,12},{15,13},{18,16},{19,... | collective-permute-start | bytes 196616 | tf_op jit(solution)/shard_map/ppermute | solution.py:27
  80.3 6.2 %collective-permute-start.13 = (f32[32,4,128]{2,1,0:T(4,128)S(1)}, f32[32,4,128]{2,1,0:T(4,128)S(1)}, u32[]{:S(2)}, u32[]{:S(2)}) collective-permute-start(f32[32,4,128]{2,1,0:T(4,128)S(1)} %get-tuple-element.256), channel_id=1, source_target_pairs={{2,0},{3,1},{6,4},{7,5},{10,8},{11,9},{14,12},{15,13},{18,16},{19,... | collective-permute-start | bytes 196616 | tf_op jit(solution)/shard_map/ppermute | solution.py:27
  94.4 6.2 %collective-permute-start.17 = (f32[32,4,128]{2,1,0:T(4,128)S(1)}, f32[32,4,128]{2,1,0:T(4,128)S(1)}, u32[]{:S(2)}, u32[]{:S(2)}) collective-permute-start(f32[32,4,128]{2,1,0:T(4,128)S(1)} %get-tuple-element.254), channel_id=1, source_target_pairs={{2,0},{3,1},{6,4},{7,5},{10,8},{11,9},{14,12},{15,13},{18,16},{19,... | collective-permute-start | bytes 196616 | tf_op jit(solution)/shard_map/ppermute | solution.py:27
  113.0 6.2 %collective-permute-start.21 = (f32[32,4,128]{2,1,0:T(4,128)S(1)}, f32[32,4,128]{2,1,0:T(4,128)S(1)}, u32[]{:S(2)}, u32[]{:S(2)}) collective-permute-start(f32[32,4,128]{2,1,0:T(4,128)S(1)} %get-tuple-element.248), channel_id=1, source_target_pairs={{2,0},{3,1},{6,4},{7,5},{10,8},{11,9},{14,12},{15,13},{18,16},{19,... | collective-permute-start | bytes 196616 | tf_op jit(solution)/shard_map/ppermute | solution.py:27
  127.4 6.8 %collective-permute-start.25 = (f32[32,4,128]{2,1,0:T(4,128)S(1)}, f32[32,4,128]{2,1,0:T(4,128)S(1)}, u32[]{:S(2)}, u32[]{:S(2)}) collective-permute-start(f32[32,4,128]{2,1,0:T(4,128)S(1)} %get-tuple-element.246), channel_id=1, source_target_pairs={{2,0},{3,1},{6,4},{7,5},{10,8},{11,9},{14,12},{15,13},{18,16},{19,... | collective-permute-start | bytes 196616 | tf_op jit(solution)/shard_map/ppermute | solution.py:27
  134.4 7.9 %collective-permute-start.26 = (f32[32,16,4]{2,1,0:T(8,128)S(1)}, f32[32,16,4]{2,1,0:T(8,128)S(1)}, u32[]{:S(2)}, u32[]{:S(2)}) collective-permute-start(f32[32,16,4]{2,1,0:T(8,128)S(1)} %get-tuple-element.213), channel_id=1, source_target_pairs={{0,1},{2,3},{4,5},{6,7},{8,9},{10,11},{12,13},{14,15},{16,17},{18,... | collective-permute-start | bytes 24584 | tf_op jit(solution)/shard_map/ppermute | solution.py:25
  136.4 6.0 %collective-permute-start.27 = (f32[32,16,4]{2,1,0:T(8,128)S(1)}, f32[32,16,4]{2,1,0:T(8,128)S(1)}, u32[]{:S(2)}, u32[]{:S(2)}) collective-permute-start(f32[32,16,4]{2,1,0:T(8,128)S(1)} %get-tuple-element.212), channel_id=1, source_target_pairs={{1,0},{3,2},{5,4},{7,6},{9,8},{11,10},{13,12},{15,14},{17,16},{19,... | collective-permute-start | bytes 24584 | tf_op jit(solution)/shard_map/ppermute | solution.py:27
  143.8 8.7 %collective-permute-start.28 = (f32[32,4,128]{2,1,0:T(4,128)S(1)}, f32[32,4,128]{2,1,0:T(4,128)S(1)}, u32[]{:S(2)}, u32[]{:S(2)}) collective-permute-start(f32[32,4,128]{2,1,0:T(4,128)S(1)} %get-tuple-element.245), channel_id=1, source_target_pairs={{0,2},{1,3},{4,6},{5,7},{8,10},{9,11},{12,14},{13,15},{16,18},{17,... | collective-permute-start | bytes 196616 | tf_op jit(solution)/shard_map/ppermute | solution.py:25
  145.3 7.2 %collective-permute-start.29 = (f32[32,4,128]{2,1,0:T(4,128)S(1)}, f32[32,4,128]{2,1,0:T(4,128)S(1)}, u32[]{:S(2)}, u32[]{:S(2)}) collective-permute-start(f32[32,4,128]{2,1,0:T(4,128)S(1)} %get-tuple-element.244), channel_id=1, source_target_pairs={{2,0},{3,1},{6,4},{7,5},{10,8},{11,9},{14,12},{15,13},{18,16},{19,... | collective-permute-start | bytes 196616 | tf_op jit(solution)/shard_map/ppermute | solution.py:27
  146.6 9.9 %collective-permute-start.32 = (f32[32,4,128]{2,1,0:T(4,128)S(1)}, f32[32,4,128]{2,1,0:T(4,128)S(1)}, u32[]{:S(2)}, u32[]{:S(2)}) collective-permute-start(f32[32,4,128]{2,1,0:T(4,128)S(1)} %get-tuple-element.253), channel_id=1, source_target_pairs={{0,2},{1,3},{4,6},{5,7},{8,10},{9,11},{12,14},{13,15},{16,18},{17,... | collective-permute-start | bytes 196616 | tf_op jit(solution)/shard_map/ppermute | solution.py:25
  151.2 6.3 %collective-permute-start.33 = (f32[32,4,128]{2,1,0:T(4,128)S(1)}, f32[32,4,128]{2,1,0:T(4,128)S(1)}, u32[]{:S(2)}, u32[]{:S(2)}) collective-permute-start(f32[32,4,128]{2,1,0:T(4,128)S(1)} %get-tuple-element.252), channel_id=1, source_target_pairs={{2,0},{3,1},{6,4},{7,5},{10,8},{11,9},{14,12},{15,13},{18,16},{19,... | collective-permute-start | bytes 196616 | tf_op jit(solution)/shard_map/ppermute | solution.py:27
  160.8 5.9 %collective-permute-start.34 = (f32[32,16,4]{2,1,0:T(8,128)S(1)}, f32[32,16,4]{2,1,0:T(8,128)S(1)}, u32[]{:S(2)}, u32[]{:S(2)}) collective-permute-start(f32[32,16,4]{2,1,0:T(8,128)S(1)} %get-tuple-element.225), channel_id=1, source_target_pairs={{0,1},{2,3},{4,5},{6,7},{8,9},{10,11},{12,13},{14,15},{16,17},{18,... | collective-permute-start | bytes 24584 | tf_op jit(solution)/shard_map/ppermute | solution.py:25
  208.1 7.6 %collective-permute-start.36 = (f32[32,4,128]{2,1,0:T(4,128)S(1)}, f32[32,4,128]{2,1,0:T(4,128)S(1)}, u32[]{:S(2)}, u32[]{:S(2)}) collective-permute-start(f32[32,4,128]{2,1,0:T(4,128)S(1)} %get-tuple-element.243), channel_id=1, source_target_pairs={{0,2},{1,3},{4,6},{5,7},{8,10},{9,11},{12,14},{13,15},{16,18},{17,... | collective-permute-start | bytes 196616 | tf_op jit(solution)/shard_map/ppermute | solution.py:25
  211.8 6.2 %collective-permute-start.37 = (f32[32,4,128]{2,1,0:T(4,128)S(1)}, f32[32,4,128]{2,1,0:T(4,128)S(1)}, u32[]{:S(2)}, u32[]{:S(2)}) collective-permute-start(f32[32,4,128]{2,1,0:T(4,128)S(1)} %get-tuple-element.242), channel_id=1, source_target_pairs={{2,0},{3,1},{6,4},{7,5},{10,8},{11,9},{14,12},{15,13},{18,16},{19,... | collective-permute-start | bytes 196616 | tf_op jit(solution)/shard_map/ppermute | solution.py:27
  (28 other events, 109.3 us)
Sparse Core Ops, SparseCore 0:
  160.8 37.5 all-reduce.12
where the time goes:
time: 233 us; the launch traced here: 232 us
  starting transfers between devices  74 us (32%)
  waiting for transfers between devices  63 us (27%)
  other arithmetic  45.3 us (19%)
  blocking collectives  19.9 us (9%)
  between operations  19.5 us (8%)
  local copies, waits for them, and re-layouts  10.1 us (4%)
    ppermute x20, starting transfers between devices, padded_2(): lax.ppermute(tail, axis, [(i, (i + 1) % count) for i in range(ends)])  47.7 us
    psum x1, waiting for transfers between devices, shards(): grad_all, illum_all = lax.psum((grad, illum), 'shots')  31.3 us
    ppermute x20, waiting for transfers between devices, padded_2(): lax.ppermute(head, axis, [((i + 1) % count, i) for i in range(ends)])  29.7 us
    ppermute x20, starting transfers between devices, padded_2(): lax.ppermute(head, axis, [((i + 1) % count, i) for i in range(ends)])  26.2 us
    scatter-add x10, other arithmetic, place_local(): flat = jnp.zeros((rows * cols,), jnp.float32).at[spots].add(kept)  24.9 us
    all_gather x1, blocking collectives, shards(): full_vel = lax.all_gather(velocity, 'shots', axis=0, tiled=True)  13.6 us
    concatenate x30, other arithmetic, padded_2(): jnp.concatenate([lax.ppermute(tail, axis, [(i, (i + 1) % count) for i in...  8.09 us
    pmax x1, blocking collectives, shards(): peak = lax.pmax(jnp.max(jnp.abs(precond)), ('dom', 'sub'))  6.3 us
  transfers between devices with their start and end apart: 41, of which 16 were waited for; matrix products, arithmetic and copies ran while one was open for 14% of the time, Pallas kernels for 0%

commit v1 on v0

--- a/solution.py
+++ b/solution.py
@@ -2,6 +2,7 @@
 import jax.numpy as jnp
 from jax import lax
 from jax.sharding import PartitionSpec as P
+from jax.lax import axis_index, axis_size, ppermute
 
 NF = 4
 NFIN = 2
@@ -75,7 +76,25 @@
     velocity, wave_prev, wave_now, adj_next, adj_now, sponge, wavelet, src_pos, rec_pos, observed
 ):
     depth, rows, cols = sponge.shape
-    full_vel = lax.all_gather(velocity, "shots", axis=0, tiled=True)
+    local_next, plain, a_next = (axis_size("shots"), axis_index("shots"), velocity.shape[0])
+    all_blocks = [(dev_j, (dev_j + 1) % local_next) for dev_j in range(local_next)]
+    table = [(dev_j, (dev_j - 1) % local_next) for dev_j in range(local_next)]
+    full_vel = jnp.zeros(
+        (*velocity.shape[:0], local_next * a_next, *velocity.shape[0 + 1 :]), velocity.dtype
+    )
+    arr_now = p_next = velocity
+    full_vel = lax.dynamic_update_slice_in_dim(full_vel, velocity, plain * a_next, axis=0)
+    newest = local_next // 2
+    for c in range(1, newest + 1):
+        arr_now = ppermute(arr_now, axis_name="shots", perm=all_blocks)
+        full_vel = lax.dynamic_update_slice_in_dim(
+            full_vel, arr_now, (plain - c) % local_next * a_next, axis=0
+        )
+        if c < local_next - newest:
+            p_next = ppermute(p_next, "shots", perm=table)
+            full_vel = lax.dynamic_update_slice_in_dim(
+                full_vel, p_next, (plain + c) % local_next * a_next, axis=0
+            )
     kappa = full_vel * full_vel
     damp = damp_rate * sponge.astype(jnp.float32)
     amps = wavelet[0]

time: 233 us -> 225 us (0.966)
  blocking collectives: 19.9 us -> 6.3 us
  starting transfers between devices: 74 us -> 77.7 us
    all_gather x1 -> x0, blocking collectives: 13.6 us -> none  [shards(): full_vel = lax.all_gather(velocity, 'shots', axis=0, tiled=True)]
    ppermute x0 -> x3, starting transfers between devices: none -> 5.26 us  [the longest x2 3.16 us: shards(): arr_now = ppermute(arr_now, axis_name='shots', perm=all_blocks)]
  transfers between devices with their start and end apart: 41 -> 44, of which waited for: 16 -> 17; matrix products, arithmetic and copies ran while one was open for 14% -> 15% of each run, Pallas kernels for 0% -> 0%
where the time goes in v1:
time: 225 us; the launch traced here: 224 us
  starting transfers between devices  77.7 us (35%)
  waiting for transfers between devices  63.5 us (28%)
  other arithmetic  45.6 us (20%)
  between operations  19.7 us (9%)
  local copies, waits for them, and re-layouts  10.9 us (5%)
  blocking collectives  6.3 us (3%)
    ppermute x20, starting transfers between devices, padded_2(): lax.ppermute(tail, axis, [(i, (i + 1) % count) for i in range(ends)])  46.2 us
    psum x1, waiting for transfers between devices, shards(): grad_all, illum_all = lax.psum((grad, illum), 'shots')  31.6 us
    ppermute x20, waiting for transfers between devices, padded_2(): lax.ppermute(head, axis, [((i + 1) % count, i) for i in range(ends)])  30 us
    ppermute x20, starting transfers between devices, padded_2(): lax.ppermute(head, axis, [((i + 1) % count, i) for i in range(ends)])  26.2 us
    scatter-add x10, other arithmetic, place_local(): flat = jnp.zeros((rows * cols,), jnp.float32).at[spots].add(kept)  25.2 us
    concatenate x30, other arithmetic, padded_2(): jnp.concatenate([lax.ppermute(tail, axis, [(i, (i + 1) % count) for i in...  8.1 us
    pmax x1, blocking collectives, shards(): peak = lax.pmax(jnp.max(jnp.abs(precond)), ('dom', 'sub'))  6.3 us
    add x10, other arithmetic, advance(): numer = 2.0 * now - (1.0 - damp) * before + kappa * lap  6.14 us
  transfers between devices with their start and end apart: 44, of which 17 were waited for; matrix products, arithmetic and copies ran while one was open for 15% of the time, Pallas kernels for 0%

profile of v1, /device:TPU:0, one launch (start us, length us, event | category | flops | bytes accessed | tf_op | source)
XLA Modules:
  0.0 223.8 jit_solution(8044189894516013778)
XLA Ops:
  7.2 3.1 %collective-permute-start = (f32[8,8,128]{2,1,0:T(8,128)}, f32[8,8,128]{2,1,0:T(8,128)S(1)}, u32[]{:S(2)}, u32[]{:S(2)}) collective-permute-start(f32[8,8,128]{2,1,0:T(8,128)} %param.42), channel_id=1, source_target_pairs={{0,4},{4,8},{8,12},{12,0},{1,5},{5,9},{9,13},{13,1},{2,6},{6,10},{... | collective-permute-start | bytes 98312 | tf_op jit(solution)/shard_map/ppermute | solution.py:89
  13.3 3.6 %collective-permute-start.7 = (f32[32,4,128]{2,1,0:T(4,128)S(1)}, f32[32,4,128]{2,1,0:T(4,128)S(1)}, u32[]{:S(2)}, u32[]{:S(2)}) collective-permute-start(f32[32,4,128]{2,1,0:T(4,128)S(1)} %get-tuple-element.261), channel_id=1, source_target_pairs={{0,2},{1,3},{4,6},{5,7},{8,10},{9,11},{12,14},{13,15},{16,18},{17,... | collective-permute-start | bytes 196616 | tf_op jit(solution)/shard_map/ppermute | solution.py:26
  18.2 4.5 %collective-permute-start.3 = (f32[32,4,128]{2,1,0:T(4,128)S(1)}, f32[32,4,128]{2,1,0:T(4,128)S(1)}, u32[]{:S(2)}, u32[]{:S(2)}) collective-permute-start(f32[32,4,128]{2,1,0:T(4,128)S(1)} %get-tuple-element.251), channel_id=1, source_target_pairs={{0,2},{1,3},{4,6},{5,7},{8,10},{9,11},{12,14},{13,15},{16,18},{17,... | collective-permute-start | bytes 196616 | tf_op jit(solution)/shard_map/ppermute | solution.py:26
  30.6 2.7 %fusion.344 = f32[1024]{0:T(1024)S(1)} fusion(f32[1024]{0:T(1024)S(1)} %broadcast.402.clone, s32[]{:T(128)} %bitcast.12, pred[1]{0:T(512)(128)(4,1)} %get-tuple-element.275, f32[1,1]{1,0:T(1,128)} %get-tuple-element.270, s32[1]{0:T(128)} %compare_select_fusion.1), kind=kLoop, calls=%fused_computation.689 | loop fusion | flops 5 | bytes 525 | tf_op jit(solution)/shard_map/scatter-add | solution.py:71
  33.3 2.6 %fusion.342 = f32[1024]{0:T(1024)S(1)} fusion(f32[1024]{0:T(1024)S(1)} %broadcast.402.clone.1, s32[]{:T(128)} %bitcast.12, pred[1]{0:T(512)(128)(4,1)} %get-tuple-element.275, f32[1,1]{1,0:T(1,128)} %get-tuple-element.269, s32[1]{0:T(128)} %compare_select_fusion.1), kind=kLoop, calls=%fused_computation.686 | loop fusion | flops 5 | bytes 525 | tf_op jit(solution)/shard_map/scatter-add | solution.py:71
  35.9 2.7 %fusion.340 = f32[1024]{0:T(1024)S(1)} fusion(f32[1024]{0:T(1024)S(1)} %broadcast.402.clone.2, s32[]{:T(128)} %bitcast.12, pred[1]{0:T(512)(128)(4,1)} %get-tuple-element.275, f32[1,1]{1,0:T(1,128)} %get-tuple-element.268, s32[1]{0:T(128)} %compare_select_fusion.1), kind=kLoop, calls=%fused_computation.683 | loop fusion | flops 5 | bytes 525 | tf_op jit(solution)/shard_map/scatter-add | solution.py:71
  38.6 2.6 %fusion.338 = f32[1024]{0:T(1024)S(1)} fusion(f32[1024]{0:T(1024)S(1)} %broadcast.402.clone.3, s32[]{:T(128)} %bitcast.12, pred[1]{0:T(512)(128)(4,1)} %get-tuple-element.275, f32[1,1]{1,0:T(1,128)} %get-tuple-element.267, s32[1]{0:T(128)} %compare_select_fusion.1), kind=kLoop, calls=%fused_computation.680 | loop fusion | flops 5 | bytes 525 | tf_op jit(solution)/shard_map/scatter-add | solution.py:71
  44.2 3.1 %collective-permute-start.9 = (f32[32,16,4]{2,1,0:T(8,128)S(1)}, f32[32,16,4]{2,1,0:T(8,128)S(1)}, u32[]{:S(2)}, u32[]{:S(2)}) collective-permute-start(f32[32,16,4]{2,1,0:T(8,128)S(1)} %get-tuple-element.241), channel_id=1, source_target_pairs={{0,1},{2,3},{4,5},{6,7},{8,9},{10,11},{12,13},{14,15},{16,17},{18,... | collective-permute-start | bytes 24584 | tf_op jit(solution)/shard_map/ppermute | solution.py:26
  52.2 4.4 %collective-permute-start.11 = (f32[32,4,128]{2,1,0:T(4,128)S(1)}, f32[32,4,128]{2,1,0:T(4,128)S(1)}, u32[]{:S(2)}, u32[]{:S(2)}) collective-permute-start(f32[32,4,128]{2,1,0:T(4,128)S(1)} %get-tuple-element.259), channel_id=1, source_target_pairs={{0,2},{1,3},{4,6},{5,7},{8,10},{9,11},{12,14},{13,15},{16,18},{17,... | collective-permute-start | bytes 196616 | tf_op jit(solution)/shard_map/ppermute | solution.py:26
  58.9 4.5 %collective-permute-done.12 = f32[32,4,128]{2,1,0:T(4,128)S(1)} collective-permute-done((f32[32,4,128]{2,1,0:T(4,128)S(1)}, f32[32,4,128]{2,1,0:T(4,128)S(1)}, u32[]{:S(2)}, u32[]{:S(2)}) %collective-permute-start.12) | collective-permute-done | bytes 65568 | tf_op jit(solution)/shard_map/ppermute | solution.py:28
  74.6 3.5 %collective-permute-done.16 = f32[32,4,128]{2,1,0:T(4,128)S(1)} collective-permute-done((f32[32,4,128]{2,1,0:T(4,128)S(1)}, f32[32,4,128]{2,1,0:T(4,128)S(1)}, u32[]{:S(2)}, u32[]{:S(2)}) %collective-permute-start.16) | collective-permute-done | bytes 65568 | tf_op jit(solution)/shard_map/ppermute | solution.py:28
  88.7 3.5 %collective-permute-done.20 = f32[32,4,128]{2,1,0:T(4,128)S(1)} collective-permute-done((f32[32,4,128]{2,1,0:T(4,128)S(1)}, f32[32,4,128]{2,1,0:T(4,128)S(1)}, u32[]{:S(2)}, u32[]{:S(2)}) %collective-permute-start.20) | collective-permute-done | bytes 65568 | tf_op jit(solution)/shard_map/ppermute | solution.py:28
  100.6 2.3 %scatter_custom_fusion = f32[1024]{0:T(1024)S(1)} fusion(s32[256]{0:T(256)S(1)} %bitcast.109, f32[256]{0:T(256)S(1)} %get-tuple-element.274, f32[]{:T(128)} %constant.427.clone.1), kind=kCustom, calls=%fused_computation.650 | custom fusion | flops 256 | bytes 4100 | tf_op jit(solution)/shard_map/scatter-add | solution.py:71
  106.7 4.1 %collective-permute-done.24 = f32[32,4,128]{2,1,0:T(4,128)S(1)} collective-permute-done((f32[32,4,128]{2,1,0:T(4,128)S(1)}, f32[32,4,128]{2,1,0:T(4,128)S(1)}, u32[]{:S(2)}, u32[]{:S(2)}) %collective-permute-start.24) | collective-permute-done | bytes 65568 | tf_op jit(solution)/shard_map/ppermute | solution.py:28
  113.7 2.3 %scatter_custom_fusion.1 = f32[1024]{0:T(1024)S(1)} fusion(s32[256]{0:T(256)S(1)} %bitcast.110, f32[256]{0:T(256)S(1)} %get-tuple-element.273, f32[]{:T(128)} %constant.427.clone.1), kind=kCustom, calls=%fused_computation.648 | custom fusion | flops 256 | bytes 4100 | tf_op jit(solution)/shard_map/scatter-add | solution.py:71
  121.3 4.5 %collective-permute-done.28 = f32[32,4,128]{2,1,0:T(4,128)S(1)} collective-permute-done((f32[32,4,128]{2,1,0:T(4,128)S(1)}, f32[32,4,128]{2,1,0:T(4,128)S(1)}, u32[]{:S(2)}, u32[]{:S(2)}) %collective-permute-start.28) | collective-permute-done | bytes 65568 | tf_op jit(solution)/shard_map/ppermute | solution.py:28
  129.3 2.3 %scatter_custom_fusion.3 = f32[1024]{0:T(1024)S(1)} fusion(s32[256]{0:T(256)S(1)} %bitcast.111, f32[256]{0:T(256)S(1)} %get-tuple-element.200, f32[]{:T(128)} %constant.427.clone.1), kind=kCustom, calls=%fused_computation.644 | custom fusion | flops 256 | bytes 4100 | tf_op jit(solution)/shard_map/scatter-add | solution.py:71
  138.2 4.5 %collective-permute-start.35 = (f32[32,4,128]{2,1,0:T(4,128)S(1)}, f32[32,4,128]{2,1,0:T(4,128)S(1)}, u32[]{:S(2)}, u32[]{:S(2)}) collective-permute-start(f32[32,4,128]{2,1,0:T(4,128)S(1)} %get-tuple-element.253), channel_id=1, source_target_pairs={{0,2},{1,3},{4,6},{5,7},{8,10},{9,11},{12,14},{13,15},{16,18},{17,... | collective-permute-start | bytes 196616 | tf_op jit(solution)/shard_map/ppermute | solution.py:26
  144.3 2.3 %collective-permute-start.33 = (f32[32,16,4]{2,1,0:T(8,128)S(1)}, f32[32,16,4]{2,1,0:T(8,128)S(1)}, u32[]{:S(2)}, u32[]{:S(2)}) collective-permute-start(f32[32,16,4]{2,1,0:T(8,128)S(1)} %get-tuple-element.209), channel_id=1, source_target_pairs={{0,1},{2,3},{4,5},{6,7},{8,9},{10,11},{12,13},{14,15},{16,17},{18,... | collective-permute-start | bytes 24584 | tf_op jit(solution)/shard_map/ppermute | solution.py:26
  155.8 2.7 %fusion.336 = f32[1024]{0:T(1024)S(1)} fusion(f32[1024]{0:T(1024)S(1)} %broadcast.402.clone.4, s32[]{:T(128)} %bitcast.12, pred[1]{0:T(512)(128)(4,1)} %get-tuple-element.275, f32[1,1]{1,0:T(1,128)} %get-tuple-element.271, s32[1]{0:T(128)} %compare_select_fusion.1), kind=kLoop, calls=%fused_computation.677 | loop fusion | flops 5 | bytes 525 | tf_op jit(solution)/shard_map/scatter-add | solution.py:71
  158.8 31.6 %all-reduce.13.cloned.1.call-done = (f32[32,8,128]{2,1,0:T(8,128)}, f32[32,8,128]{2,1,0:T(8,128)}) async-done(((f32[32,8,128]{2,1,0:T(8,128)}, f32[32,8,128]{2,1,0:T(8,128)}), (f32[32,8,128]{2,1,0:T(8,128)}, f32[32,8,128]{2,1,0:T(8,128)})) %all-reduce.13.cloned.1.call-update) | async-done | bytes 262160 | tf_op jit(solution)/shard_map/psum | solution.py:123
  192.4 6.3 %pmax.7 = f32[]{:T(128)} all-reduce(f32[]{:T(128)} %abs_reduce_fusion), channel_id=1, replica_groups=mesh['groups'=2,'shots'=4,'dom'=2,'sub'=2] {'dom','sub'}, use_global_device_ids=true, to_apply=%region_7.8 | all-reduce | flops 1 | bytes 8 | tf_op jit(solution)/shard_map/pmax | solution.py:125
  200.1 3.6 %collective-permute-start.39 = (f32[32,4,128]{2,1,0:T(4,128)S(1)}, f32[32,4,128]{2,1,0:T(4,128)S(1)}, u32[]{:S(2)}, u32[]{:S(2)}) collective-permute-start(f32[32,4,128]{2,1,0:T(4,128)S(1)} %get-tuple-element.243), channel_id=1, source_target_pairs={{0,2},{1,3},{4,6},{5,7},{8,10},{9,11},{12,14},{13,15},{16,18},{17,... | collective-permute-start | bytes 196616 | tf_op jit(solution)/shard_map/ppermute | solution.py:26
  205.1 2.6 %fusion.334 = f32[1024]{0:T(1024)S(1)} fusion(f32[1024]{0:T(1024)S(1)} %broadcast.402.clone.5, s32[]{:T(128)} %bitcast.12, pred[1]{0:T(512)(128)(4,1)} %get-tuple-element.275, f32[1,1]{1,0:T(1,128)} %get-tuple-element.266, s32[1]{0:T(128)} %compare_select_fusion.1), kind=kLoop, calls=%fused_computation.674 | loop fusion | flops 5 | bytes 525 | tf_op jit(solution)/shard_map/scatter-add | solution.py:71
  (208 shorter events, 94.2 us)
Async XLA Ops:
  7.2 183.2 %all-reduce.13.cloned.1.call-start = ((), (), s32[]{:S(2)}) async-start(), calls=%async_computation | async-start | bytes 524288 | tf_op jit(solution)/shard_map/psum | solution.py:123
  7.2 34.0 %collective-permute-start = (f32[8,8,128]{2,1,0:T(8,128)}, f32[8,8,128]{2,1,0:T(8,128)S(1)}, u32[]{:S(2)}, u32[]{:S(2)}) collective-permute-start(f32[8,8,128]{2,1,0:T(8,128)} %param.42), channel_id=1, source_target_pairs={{0,4},{4,8},{8,12},{12,0},{1,5},{5,9},{9,13},{13,1},{2,6},{6,10},{... | collective-permute-start | bytes 98312 | tf_op jit(solution)/shard_map/ppermute | solution.py:89
  10.3 32.2 %collective-permute-start.1 = (f32[8,8,128]{2,1,0:T(8,128)}, f32[8,8,128]{2,1,0:T(8,128)S(1)}, u32[]{:S(2)}, u32[]{:S(2)}) collective-permute-start(f32[8,8,128]{2,1,0:T(8,128)} %param.42), channel_id=1, source_target_pairs={{0,12},{4,0},{8,4},{12,8},{1,13},{5,1},{9,5},{13,9},{2,14},{6,2},{... | collective-permute-start | bytes 98312 | tf_op jit(solution)/shard_map/ppermute | solution.py:94
  13.3 29.3 %collective-permute-start.7 = (f32[32,4,128]{2,1,0:T(4,128)S(1)}, f32[32,4,128]{2,1,0:T(4,128)S(1)}, u32[]{:S(2)}, u32[]{:S(2)}) collective-permute-start(f32[32,4,128]{2,1,0:T(4,128)S(1)} %get-tuple-element.261), channel_id=1, source_target_pairs={{0,2},{1,3},{4,6},{5,7},{8,10},{9,11},{12,14},{13,15},{16,18},{17,... | collective-permute-start | bytes 196616 | tf_op jit(solution)/shard_map/ppermute | solution.py:26
  16.9 25.8 %collective-permute-start.8 = (f32[32,4,128]{2,1,0:T(4,128)S(1)}, f32[32,4,128]{2,1,0:T(4,128)S(1)}, u32[]{:S(2)}, u32[]{:S(2)}) collective-permute-start(f32[32,4,128]{2,1,0:T(4,128)S(1)} %get-tuple-element.260), channel_id=1, source_target_pairs={{2,0},{3,1},{6,4},{7,5},{10,8},{11,9},{14,12},{15,13},{18,16},{19,... | collective-permute-start | bytes 196616 | tf_op jit(solution)/shard_map/ppermute | solution.py:28
  18.2 29.0 %collective-permute-start.3 = (f32[32,4,128]{2,1,0:T(4,128)S(1)}, f32[32,4,128]{2,1,0:T(4,128)S(1)}, u32[]{:S(2)}, u32[]{:S(2)}) collective-permute-start(f32[32,4,128]{2,1,0:T(4,128)S(1)} %get-tuple-element.251), channel_id=1, source_target_pairs={{0,2},{1,3},{4,6},{5,7},{8,10},{9,11},{12,14},{13,15},{16,18},{17,... | collective-permute-start | bytes 196616 | tf_op jit(solution)/shard_map/ppermute | solution.py:26
  41.2 6.1 %collective-permute-start.4 = (f32[32,4,128]{2,1,0:T(4,128)S(1)}, f32[32,4,128]{2,1,0:T(4,128)S(1)}, u32[]{:S(2)}, u32[]{:S(2)}) collective-permute-start(f32[32,4,128]{2,1,0:T(4,128)S(1)} %get-tuple-element.250), channel_id=1, source_target_pairs={{2,0},{3,1},{6,4},{7,5},{10,8},{11,9},{14,12},{15,13},{18,16},{19,... | collective-permute-start | bytes 196616 | tf_op jit(solution)/shard_map/ppermute | solution.py:28
  42.6 7.6 %collective-permute-start.2 = (f32[8,8,128]{2,1,0:T(8,128)S(1)}, f32[8,8,128]{2,1,0:T(8,128)S(1)}, u32[]{:S(2)}, u32[]{:S(2)}) collective-permute-start(f32[8,8,128]{2,1,0:T(8,128)S(1)} %collective-permute-done), channel_id=1, source_target_pairs={{0,4},{4,8},{8,12},{12,0},{1,5},{5,9},{9,13},{13,1},{2,6},{6,10},{... | collective-permute-start | bytes 98312 | tf_op jit(solution)/shard_map/ppermute | solution.py:89
  42.9 7.4 %collective-permute-start.10 = (f32[32,16,4]{2,1,0:T(8,128)S(1)}, f32[32,16,4]{2,1,0:T(8,128)S(1)}, u32[]{:S(2)}, u32[]{:S(2)}) collective-permute-start(f32[32,16,4]{2,1,0:T(8,128)S(1)} %get-tuple-element.240), channel_id=1, source_target_pairs={{1,0},{3,2},{5,4},{7,6},{9,8},{11,10},{13,12},{15,14},{17,16},{19,... | collective-permute-start | bytes 24584 | tf_op jit(solution)/shard_map/ppermute | solution.py:28
  47.6 10.4 %collective-permute-start.5 = (f32[32,16,4]{2,1,0:T(8,128)S(1)}, f32[32,16,4]{2,1,0:T(8,128)S(1)}, u32[]{:S(2)}, u32[]{:S(2)}) collective-permute-start(f32[32,16,4]{2,1,0:T(8,128)S(1)} %get-tuple-element.221), channel_id=1, source_target_pairs={{0,1},{2,3},{4,5},{6,7},{8,9},{10,11},{12,13},{14,15},{16,17},{18,... | collective-permute-start | bytes 24584 | tf_op jit(solution)/shard_map/ppermute | solution.py:26
  48.9 9.1 %collective-permute-start.6 = (f32[32,16,4]{2,1,0:T(8,128)S(1)}, f32[32,16,4]{2,1,0:T(8,128)S(1)}, u32[]{:S(2)}, u32[]{:S(2)}) collective-permute-start(f32[32,16,4]{2,1,0:T(8,128)S(1)} %get-tuple-element.220), channel_id=1, source_target_pairs={{1,0},{3,2},{5,4},{7,6},{9,8},{11,10},{13,12},{15,14},{17,16},{19,... | collective-permute-start | bytes 24584 | tf_op jit(solution)/shard_map/ppermute | solution.py:28
  52.2 6.7 %collective-permute-start.11 = (f32[32,4,128]{2,1,0:T(4,128)S(1)}, f32[32,4,128]{2,1,0:T(4,128)S(1)}, u32[]{:S(2)}, u32[]{:S(2)}) collective-permute-start(f32[32,4,128]{2,1,0:T(4,128)S(1)} %get-tuple-element.259), channel_id=1, source_target_pairs={{0,2},{1,3},{4,6},{5,7},{8,10},{9,11},{12,14},{13,15},{16,18},{17,... | collective-permute-start | bytes 196616 | tf_op jit(solution)/shard_map/ppermute | solution.py:26
  56.6 6.7 %collective-permute-start.12 = (f32[32,4,128]{2,1,0:T(4,128)S(1)}, f32[32,4,128]{2,1,0:T(4,128)S(1)}, u32[]{:S(2)}, u32[]{:S(2)}) collective-permute-start(f32[32,4,128]{2,1,0:T(4,128)S(1)} %get-tuple-element.258), channel_id=1, source_target_pairs={{2,0},{3,1},{6,4},{7,5},{10,8},{11,9},{14,12},{15,13},{18,16},{19,... | collective-permute-start | bytes 196616 | tf_op jit(solution)/shard_map/ppermute | solution.py:28
  71.9 6.2 %collective-permute-start.16 = (f32[32,4,128]{2,1,0:T(4,128)S(1)}, f32[32,4,128]{2,1,0:T(4,128)S(1)}, u32[]{:S(2)}, u32[]{:S(2)}) collective-permute-start(f32[32,4,128]{2,1,0:T(4,128)S(1)} %get-tuple-element.256), channel_id=1, source_target_pairs={{2,0},{3,1},{6,4},{7,5},{10,8},{11,9},{14,12},{15,13},{18,16},{19,... | collective-permute-start | bytes 196616 | tf_op jit(solution)/shard_map/ppermute | solution.py:28
  86.0 6.2 %collective-permute-start.20 = (f32[32,4,128]{2,1,0:T(4,128)S(1)}, f32[32,4,128]{2,1,0:T(4,128)S(1)}, u32[]{:S(2)}, u32[]{:S(2)}) collective-permute-start(f32[32,4,128]{2,1,0:T(4,128)S(1)} %get-tuple-element.254), channel_id=1, source_target_pairs={{2,0},{3,1},{6,4},{7,5},{10,8},{11,9},{14,12},{15,13},{18,16},{19,... | collective-permute-start | bytes 196616 | tf_op jit(solution)/shard_map/ppermute | solution.py:28
  104.6 6.2 %collective-permute-start.24 = (f32[32,4,128]{2,1,0:T(4,128)S(1)}, f32[32,4,128]{2,1,0:T(4,128)S(1)}, u32[]{:S(2)}, u32[]{:S(2)}) collective-permute-start(f32[32,4,128]{2,1,0:T(4,128)S(1)} %get-tuple-element.248), channel_id=1, source_target_pairs={{2,0},{3,1},{6,4},{7,5},{10,8},{11,9},{14,12},{15,13},{18,16},{19,... | collective-permute-start | bytes 196616 | tf_op jit(solution)/shard_map/ppermute | solution.py:28
  119.0 6.8 %collective-permute-start.28 = (f32[32,4,128]{2,1,0:T(4,128)S(1)}, f32[32,4,128]{2,1,0:T(4,128)S(1)}, u32[]{:S(2)}, u32[]{:S(2)}) collective-permute-start(f32[32,4,128]{2,1,0:T(4,128)S(1)} %get-tuple-element.246), channel_id=1, source_target_pairs={{2,0},{3,1},{6,4},{7,5},{10,8},{11,9},{14,12},{15,13},{18,16},{19,... | collective-permute-start | bytes 196616 | tf_op jit(solution)/shard_map/ppermute | solution.py:28
  126.0 7.9 %collective-permute-start.29 = (f32[32,16,4]{2,1,0:T(8,128)S(1)}, f32[32,16,4]{2,1,0:T(8,128)S(1)}, u32[]{:S(2)}, u32[]{:S(2)}) collective-permute-start(f32[32,16,4]{2,1,0:T(8,128)S(1)} %get-tuple-element.213), channel_id=1, source_target_pairs={{0,1},{2,3},{4,5},{6,7},{8,9},{10,11},{12,13},{14,15},{16,17},{18,... | collective-permute-start | bytes 24584 | tf_op jit(solution)/shard_map/ppermute | solution.py:26
  135.4 8.7 %collective-permute-start.31 = (f32[32,4,128]{2,1,0:T(4,128)S(1)}, f32[32,4,128]{2,1,0:T(4,128)S(1)}, u32[]{:S(2)}, u32[]{:S(2)}) collective-permute-start(f32[32,4,128]{2,1,0:T(4,128)S(1)} %get-tuple-element.245), channel_id=1, source_target_pairs={{0,2},{1,3},{4,6},{5,7},{8,10},{9,11},{12,14},{13,15},{16,18},{17,... | collective-permute-start | bytes 196616 | tf_op jit(solution)/shard_map/ppermute | solution.py:26
  136.9 7.2 %collective-permute-start.32 = (f32[32,4,128]{2,1,0:T(4,128)S(1)}, f32[32,4,128]{2,1,0:T(4,128)S(1)}, u32[]{:S(2)}, u32[]{:S(2)}) collective-permute-start(f32[32,4,128]{2,1,0:T(4,128)S(1)} %get-tuple-element.244), channel_id=1, source_target_pairs={{2,0},{3,1},{6,4},{7,5},{10,8},{11,9},{14,12},{15,13},{18,16},{19,... | collective-permute-start | bytes 196616 | tf_op jit(solution)/shard_map/ppermute | solution.py:28
  138.2 9.9 %collective-permute-start.35 = (f32[32,4,128]{2,1,0:T(4,128)S(1)}, f32[32,4,128]{2,1,0:T(4,128)S(1)}, u32[]{:S(2)}, u32[]{:S(2)}) collective-permute-start(f32[32,4,128]{2,1,0:T(4,128)S(1)} %get-tuple-element.253), channel_id=1, source_target_pairs={{0,2},{1,3},{4,6},{5,7},{8,10},{9,11},{12,14},{13,15},{16,18},{17,... | collective-permute-start | bytes 196616 | tf_op jit(solution)/shard_map/ppermute | solution.py:26
  142.8 6.3 %collective-permute-start.36 = (f32[32,4,128]{2,1,0:T(4,128)S(1)}, f32[32,4,128]{2,1,0:T(4,128)S(1)}, u32[]{:S(2)}, u32[]{:S(2)}) collective-permute-start(f32[32,4,128]{2,1,0:T(4,128)S(1)} %get-tuple-element.252), channel_id=1, source_target_pairs={{2,0},{3,1},{6,4},{7,5},{10,8},{11,9},{14,12},{15,13},{18,16},{19,... | collective-permute-start | bytes 196616 | tf_op jit(solution)/shard_map/ppermute | solution.py:28
  200.1 7.5 %collective-permute-start.39 = (f32[32,4,128]{2,1,0:T(4,128)S(1)}, f32[32,4,128]{2,1,0:T(4,128)S(1)}, u32[]{:S(2)}, u32[]{:S(2)}) collective-permute-start(f32[32,4,128]{2,1,0:T(4,128)S(1)} %get-tuple-element.243), channel_id=1, source_target_pairs={{0,2},{1,3},{4,6},{5,7},{8,10},{9,11},{12,14},{13,15},{16,18},{17,... | collective-permute-start | bytes 196616 | tf_op jit(solution)/shard_map/ppermute | solution.py:26
  203.7 6.2 %collective-permute-start.40 = (f32[32,4,128]{2,1,0:T(4,128)S(1)}, f32[32,4,128]{2,1,0:T(4,128)S(1)}, u32[]{:S(2)}, u32[]{:S(2)}) collective-permute-start(f32[32,4,128]{2,1,0:T(4,128)S(1)} %get-tuple-element.242), channel_id=1, source_target_pairs={{2,0},{3,1},{6,4},{7,5},{10,8},{11,9},{14,12},{15,13},{18,16},{19,... | collective-permute-start | bytes 196616 | tf_op jit(solution)/shard_map/ppermute | solution.py:28
  (31 other events, 111.7 us)
Sparse Core Ops, SparseCore 0:
  152.4 37.9 all-reduce.12
